TPU v7x, 512 devices: a whole 4x4x16 slice. The times are simulated.
512 devices in a mesh: row: 4 (over x), col: 16 (over z), ch: 8 (over y, core).
Axes of the slice: x: 4, y: 4, z: 16, core: 2. Of those that a mesh axis runs over, the one named last changes fastest.
Arguments:
- features: bfloat16 [192, 256, 2048], P('ch', 'row', 'col'), may hold values from -6 to 6
- cotangent: bfloat16 [192, 256, 2048], P('ch', 'row', 'col'), may hold values from -8 to 8
- dw_kernel: float32 [192, 49], P('ch'), may hold values from -0.875 to 0.875
- dw_bias: float32 [192], P('ch'), may hold values from -1 to 1
- ln_gain: float32 [192], replicated, may hold values from 0.1 to 1.9
- ln_bias: float32 [192], replicated, may hold values from -3 to 3
- w_in: bfloat16 [192, 768], replicated, may hold values from -0.4375 to 0.4375
- in_bias: float32 [768], replicated, may hold values from -3 to 3
- w_out: bfloat16 [768, 192], replicated, may hold values from -0.21875 to 0.21875
- out_bias: float32 [192], replicated, may hold values from -3 to 3
- layer_scale: float32 [192], replicated, may hold values from 0.5 to 2
Outputs:
- output: bfloat16 [192, 256, 2048], P('ch', 'row', 'col')
- grad_input: bfloat16 [192, 256, 2048], P('ch', 'row', 'col')
- grad_w_in: float32 [192, 768], P(None, 'ch')
- grad_w_out: float32 [768, 192], P('ch')
- grad_in_bias: float32 [768], P('ch')
- grad_vectors: float32 [4, 192], replicated
- grad_conv: float32 [192, 50], P('ch')
All inputs are finite; a program needn't handle non-finite values.
Results may differ from a plain program's by a relative error of at most 0.015.
Values may be sent and summed in bfloat16 or wider, within the bound.
A program may use at most 64 MiB of HBM per device.

v0:
```python
import functools
import math

import jax
import jax.numpy as jnp
from jax import lax
from jax.experimental import pallas as pl
from jax.experimental.pallas import tpu as pltpu
from jax.sharding import PartitionSpec as P

KW = 7
HALF = 3
LANES = 128
SQRT_HALF = 0.7071067811865476
INV_SQRT_TWO_PI = 0.3989422804014327
EPSILON = 1e-06
MESH = pl.DeviceIdType.MESH
F32 = jnp.float32
BF16 = jnp.bfloat16

ERF_P = 0.3275911 * SQRT_HALF
ERF_A = (0.254829592, -0.284496736, 1.421413741, -1.453152027, 1.061405429)


def gelu_parts(v):
    bell = jnp.exp(-0.5 * v * v)
    t = 1.0 / (1.0 + ERF_P * jnp.abs(v))
    poly = 0.5 * ERF_A[4]
    for a in ERF_A[3::-1]:
        poly = poly * t + 0.5 * a
    tail = poly * t * bell
    cumul = jnp.where(v >= 0, 1.0 - tail, tail)
    return v * cumul, cumul + v * (INV_SQRT_TWO_PI * bell)


def dot(a, b):
    return jnp.dot(a, b, preferred_element_type=F32)


def dot_nt(a, b):
    return lax.dot_general(a, b, (((1,), (1,)), ((), ())), preferred_element_type=F32)


def lane_iota(rows):
    return lax.broadcasted_iota(jnp.int32, (rows, LANES), 1)


def remote(src, dst, send, recv, **where):
    return pltpu.make_async_remote_copy(
        src_ref=src, dst_ref=dst, send_sem=send, recv_sem=recv, device_id=where, device_id_type=MESH
    )


def block_kernel(
    dims,
    feat,
    cot,
    dw_kernel,
    dw_bias,
    cols,
    in_bias,
    w_in,
    w_out,
    out,
    gin,
    gw_out,
    v_out,
    t_out,
    xs,
    gs,
    wb,
    cb,
    vecs,
    edge,
    hrow,
    hedge,
    hcorner,
    edge2,
    hrow2,
    hedge2,
    hcorner2,
    stage,
    gb,
    mb,
    rm,
    rc,
    sb,
    rb,
    wa,
    wint,
    woutt,
    g1,
    g2,
    va,
    sx,
    rx,
    sv,
    rvx,
    sy,
    ry,
    svy,
    rvy,
    taps,
    st,
    rt,
    zt,
    rz,
    zs,
    h_s,
    h_r,
    h2_s,
    h2_r,
    c_s,
    c_r,
    m_s,
    m_r,
    e_s,
    e_r,
    x_s,
    x_r,
    vx_s,
    vx_r,
    y_s,
    y_r,
    vy_s,
    vy_r,
    t_s,
    t_r,
    z_s,
    z_r,
    a_s,
    a_r,
    f_s,
    f_r,
    ring,
):
    n_row, n_col, n_ch, cd, rows, chan, hid = dims
    share = rows // n_ch
    chunks = share // 2
    blk = share * cd
    pair = 2 * cd
    hb = hid // n_ch // n_row
    n_gw = hb // 8 * 3
    n_t = n_gw + 2 + cd // 8
    kb = min(256, hid)
    me_r = lax.axis_index("row")
    me_c = lax.axis_index("col")
    me = lax.axis_index("ch")
    up, down = lax.rem(me_r + n_row - 1, n_row), lax.rem(me_r + 1, n_row)
    left, right = lax.rem(me_c + n_col - 1, n_col), lax.rem(me_c + 1, n_col)

    barrier = pltpu.get_barrier_semaphore()
    near = []
    for k in range(1, n_ch):
        near.append(dict(row=me_r, col=me_c, ch=lax.rem(me + k, n_ch)))
    for k in range(1, n_row):
        near.append(dict(row=lax.rem(me_r + k, n_row), col=me_c, ch=me))
    for c in (left, right):
        for r in (me_r, up, down):
            near.append(dict(row=r, col=c, ch=me))
    for where in near:
        pl.semaphore_signal(barrier, inc=1, device_id=where, device_id_type=MESH)

    def pack_edges(src, buf):
        lane = lane_iota(cd)

        def step(t, acc):
            keep = (lane >= 4 * t) & (lane < 4 * t + 4)
            new = []
            for k in range(rows // 32):
                x = src[pl.ds(pl.multiple_of((HALF + 32 * k + t) * cd, 8), cd), :]
                new.append(jnp.where(keep, pltpu.roll(x, 4 * t, 1), acc[2 * k]))
                new.append(
                    jnp.where(keep, pltpu.roll(x, lax.rem(4 * t + 4, LANES), 1), acc[2 * k + 1])
                )
            return tuple(new)

        zero = jnp.zeros((cd, LANES), F32)
        acc = lax.fori_loop(0, 32, step, (zero,) * (2 * (rows // 32)))
        pad = jnp.zeros((edge_pitch - cd, LANES), F32)
        for k in range(rows // 32):
            for side in range(2):
                full = acc[2 * k + side]
                if edge_pitch > cd:
                    full = jnp.concatenate([full, pad], axis=0)
                buf[side, k] = full.astype(BF16)

    edge_pitch = edge.shape[2]
    n_tiles = rows // 32

    def fill_center(src):
        for q in range(n_ch):
            xs[HALF, pl.ds((HALF + q * share) * cd, blk), :] = src[pl.ds(q * blk, blk), :].astype(F32)

    fill_center(feat)
    pack_edges(xs.at[HALF], edge)

    for t in range(KW * KW):
        wb[pl.ds(t * cd, cd), :] = jnp.broadcast_to(dw_kernel[:, t : t + 1], (cd, LANES))
    cb[...] = jnp.broadcast_to(dw_bias[...], (cd, LANES))

    pl.semaphore_wait(barrier, len(near))

    def halo_copies(src, ebuf, rbuf, lbuf, cbuf, ss, rs):
        four = 4 * cd
        last = (rows - 4) * cd
        copies = [
            remote(src.at[pl.ds(0, four), :], rbuf.at[1], ss.at[0], rs.at[0], row=up, col=me_c, ch=me),
            remote(src.at[pl.ds(last, four), :], rbuf.at[0], ss.at[1], rs.at[1], row=down, col=me_c, ch=me),
            remote(ebuf.at[0], lbuf.at[1], ss.at[2], rs.at[2], row=me_r, col=left, ch=me),
            remote(ebuf.at[1], lbuf.at[0], ss.at[3], rs.at[3], row=me_r, col=right, ch=me),
        ]
        copies.append(remote(ebuf.at[0, 0], cbuf.at[1, 1], ss.at[4], rs.at[4], row=up, col=left, ch=me))
        copies.append(remote(ebuf.at[1, 0], cbuf.at[1, 0], ss.at[5], rs.at[5], row=up, col=right, ch=me))
        copies.append(
            remote(ebuf.at[0, n_tiles - 1], cbuf.at[0, 1], ss.at[6], rs.at[6], row=down, col=left, ch=me)
        )
        copies.append(
            remote(ebuf.at[1, n_tiles - 1], cbuf.at[0, 0], ss.at[7], rs.at[7], row=down, col=right, ch=me)
        )
        return copies

    halo1 = halo_copies(feat, edge, hrow, hedge, hcorner, h_s, h_r)
    for copy in halo1:
        copy.start()

    def cot_copy(k):
        q = lax.rem(me + k, n_ch)
        return remote(cot.at[q], rc.at[me], c_s.at[q], c_r.at[me], row=me_r, col=me_c, ch=q)

    def came(buf, ss, rs, q, idx=None):
        dst = buf.at[q] if idx is None else buf.at[q, idx]
        recv = rs.at[q] if idx is None else rs.at[q, idx]
        send = ss.at[q] if idx is None else ss.at[q, idx]
        return remote(dst, dst, send, recv, row=me_r, col=me_c, ch=q)

    for k in range(1, n_ch):
        cot_copy(k).start()

    eye = lambda n: (
        lax.broadcasted_iota(jnp.int32, (n, n), 0) == lax.broadcasted_iota(jnp.int32, (n, n), 1)
    ).astype(BF16)
    wa[pl.ds(0, chan), :] = w_in[...]
    bias_row = in_bias[...]
    hi = bias_row.astype(BF16).astype(F32)
    lo = bias_row - hi
    row_id = lax.broadcasted_iota(jnp.int32, (64, hid), 0)
    wa[pl.ds(chan, 64), :] = jnp.where(
        row_id == 0, jnp.broadcast_to(hi, (64, hid)), jnp.where(row_id == 1, jnp.broadcast_to(lo, (64, hid)), 0.0)
    ).astype(BF16)
    for k in range(hid // kb):
        wint[pl.ds(k * kb, kb), :] = dot_nt(eye(kb), wa[:, k * kb : (k + 1) * kb]).astype(BF16)
        woutt[:, k * kb : (k + 1) * kb] = dot_nt(eye(chan), w_out[pl.ds(k * kb, kb), :]).astype(BF16)
    for k in range(4):
        vecs[k] = jnp.broadcast_to(cols[:, k : k + 1], (chan, LANES))
    g1[...] = jnp.zeros_like(g1)
    g2[...] = jnp.zeros_like(g2)
    va[...] = jnp.zeros_like(va)
    taps[...] = jnp.zeros_like(taps)
    rc[me] = cot[me]

    def as_f32(flag):
        return jnp.where(flag, 1.0, 0.0).astype(F32)

    def shifted_copies(buf, rbuf, lbuf, cbuf):
        has_up, has_down = as_f32(me_r > 0), as_f32(me_r < n_row - 1)
        has_left, has_right = as_f32(me_c > 0), as_f32(me_c < n_col - 1)
        buf[HALF, pl.ds(0, HALF * cd), :] = rbuf[0].astype(F32)[cd:] * has_up
        buf[HALF, pl.ds((HALF + rows) * cd, HALF * cd), :] = rbuf[1].astype(F32)[: HALF * cd] * has_down
        for side, has in ((0, has_left), (1, has_right)):
            stage[side, 0] = cbuf[0, side].astype(F32)[:cd] * (has * has_up)
            for k in range(n_tiles):
                stage[side, 1 + k] = lbuf[side, k].astype(F32)[:cd] * has
            stage[side, 1 + n_tiles] = cbuf[1, side].astype(F32)[:cd] * (has * has_down)
        lane = lane_iota(cd)

        def one_row(i, carry):
            at = i + 32 - HALF
            tile, t = lax.div(at, 32), lax.rem(at, 32)
            halo = jnp.where(
                lane < 64,
                pltpu.roll(stage[1, tile], lax.rem(LANES - 4 * t, LANES), 1),
                pltpu.roll(stage[0, tile], 124 - 4 * t, 1),
            )
            where = pl.ds(pl.multiple_of(i * cd, 8), cd)
            x = buf[HALF, where, :]
            for s in range(1, HALF + 1):
                buf[HALF + s, where, :] = pltpu.roll(jnp.where(lane < s, halo, x), LANES - s, 1)
                buf[HALF - s, where, :] = pltpu.roll(jnp.where(lane >= LANES - s, halo, x), s, 1)
            return carry

        lax.fori_loop(0, rows + 2 * HALF, one_row, 0)

    for copy in halo1:
        copy.wait_recv()

    reach = []
    r = 2
    while r < n_col // 2:
        reach.append(r)
        r *= 2

    def tell(i):
        for step in (reach[i], n_col - reach[i]):
            pl.semaphore_signal(
                ring.at[i],
                inc=1,
                device_id=dict(row=me_r, col=lax.rem(me_c + step, n_col), ch=me),
                device_id_type=MESH,
            )

    if reach:
        tell(0)

    shifted_copies(xs, hrow, hedge, hcorner)

    def conv(buf, base, start, flip):
        acc = start
        for b in range(KW):
            for a in range(KW):
                tap = (KW - 1 - a) * KW + KW - 1 - b if flip else a * KW + b
                w = wb[pl.ds(tap * cd, cd), :]
                x = buf[b, pl.ds(pl.multiple_of((base + a) * cd, 8), blk), :]
                acc = acc + jnp.concatenate([w] * share, axis=0) * x
        return acc

    def mix_copy(q):
        return remote(mb.at[q], rm.at[me], m_s.at[q], m_r.at[me], row=me_r, col=me_c, ch=q)

    def forward(k, carry):
        q = lax.rem(me + 1 + k, n_ch)
        start = jnp.concatenate([cb[...]] * share, axis=0)
        mb[q] = conv(xs, q * share, start, False).astype(BF16)

        @pl.when(k < n_ch - 1)
        def _():
            mix_copy(q).start()

        return carry

    lax.fori_loop(0, n_ch, forward, 0)
    rm[me] = mb[me]

    for k in range(1, n_ch):
        q = lax.rem(me + k, n_ch)
        came(rc, c_s, c_r, q).wait_recv()
        came(rm, m_s, m_r, q).wait_recv()

    if len(reach) > 1:
        pl.semaphore_wait(ring.at[0], 2)
        tell(1)

    px = 2 * LANES
    ones_rows = (lax.broadcasted_iota(jnp.int32, (64, px), 0) < 2).astype(F32).astype(BF16)

    def wide(v):
        return jnp.concatenate([v, v], axis=1)

    def gather(buf, at):
        parts = []
        for q in range(n_ch):
            both = buf[q, at, :].astype(F32)
            parts.append(jnp.concatenate([both[:cd], both[cd:]], axis=1))
        return jnp.concatenate(parts, axis=0)

    def exit_copy(q, k):
        return remote(sb.at[q, k], rb.at[me, k], e_s.at[q, k], e_r.at[me, k], row=me_r, col=me_c, ch=q)

    def fold(v):
        return v[:, :LANES] + v[:, LANES:]

    def chunk(k, carry):
        at = pl.ds(pl.multiple_of(k * pair, 16), pair)
        gain, shift, outb, scale = (wide(vecs[i]) for i in range(4))
        values = gather(rm, at)
        centre = jnp.mean(values, axis=0, keepdims=True)
        away = values - centre
        inv_std = lax.rsqrt(jnp.mean(away * away, axis=0, keepdims=True) + EPSILON)
        normed = away * inv_std
        scaled = (normed * gain + shift).astype(BF16)
        scaled = jnp.concatenate([scaled, ones_rows], axis=0)
        cotan = gather(rc, at)
        cots = (cotan * scale).astype(BF16)
        projected = jnp.zeros((chan, px), F32)
        grad_scaled = jnp.zeros((chan, px), F32)
        for j in range(hid // kb):
            rows_j = pl.ds(j * kb, kb)
            act, slope = gelu_parts(dot(wint[rows_j, :], scaled))
            hidden = act.astype(BF16)
            grad_hidden = (dot(w_out[rows_j, :], cots) * slope).astype(BF16)
            projected = projected + dot(woutt[:, j * kb : (j + 1) * kb], hidden)
            grad_scaled = grad_scaled + dot(w_in[:, j * kb : (j + 1) * kb], grad_hidden)
            g1[rows_j, :] += dot_nt(grad_hidden, scaled)
            g2[rows_j, :] += dot_nt(hidden, cots)
        projected = projected + outb
        branch = scale * projected
        va[0] += fold(cots.astype(F32))
        va[1] += fold(grad_scaled * normed)
        va[2] += fold(grad_scaled)
        va[3] += fold(cotan * projected)
        gn = grad_scaled * gain
        m1 = jnp.mean(gn, axis=0, keepdims=True)
        m2 = jnp.mean(gn * normed, axis=0, keepdims=True)
        gm = (gn - m1 - normed * m2) * inv_std
        for q in range(n_ch):
            for i, v in enumerate((branch, gm)):
                piece = v[q * cd : (q + 1) * cd]
                sb[q, k, pl.ds(i * pair, pair), :] = jnp.concatenate(
                    [piece[:, :LANES], piece[:, LANES:]], axis=0
                ).astype(BF16)
        for d in range(1, n_ch):
            exit_copy(lax.rem(me + d, n_ch), k).start()
        rb[me, k] = sb[me, k]
        return carry

    lax.fori_loop(0, chunks, chunk, 0)

    half = lane_iota(pair_rows := 2 * hb) < 64
    for r in range(n_row):
        for q in range(0, n_ch, 2):
            at = [(q + i) * hb * n_row + r * hb for i in range(2)]
            a, b = (
                jnp.concatenate([g[pl.ds(at[i], hb), :] for i in range(2)], axis=0) for g in (g1, g2)
            )
            b_hi = pltpu.roll(
                jnp.concatenate([b[:, LANES:], jnp.zeros((pair_rows, 2 * LANES - chan), F32)], axis=1), 64, 1
            )
            sx[r, pl.ds(q * hb, pair_rows), :] = jnp.concatenate(
                [a[:, :LANES], b[:, :LANES], jnp.where(half, a[:, LANES:], b_hi)], axis=1
            ).astype(BF16)
    lane_c = lane_iota(chan)
    table = jnp.zeros((chan, LANES), F32)
    for i in range(4):
        table = jnp.where(lane_c == i, jnp.sum(va[i], axis=1, keepdims=True), table)
    for i in range(hid // chan):
        part = pltpu.roll(g1[pl.ds(i * chan, chan), LANES:], LANES - 64 + 4 + i, 1)
        table = jnp.where(lane_c == 4 + i, part, table)
    table = jnp.concatenate([table, jnp.zeros((2 * LANES - chan, LANES), F32)], axis=0)
    sv[...] = table.T[:8]

    def x_copies(k):
        r = lax.rem(me_r + k, n_row)
        return (
            remote(sx.at[r], rx.at[me_r], x_s.at[r], x_r.at[me_r], row=r, col=me_c, ch=me),
            remote(sv, rvx.at[me_r], vx_s.at[r], vx_r.at[me_r], row=r, col=me_c, ch=me),
        )

    for k in range(1, n_row):
        for copy in x_copies(k):
            copy.start()
    rx[me_r] = sx[me_r]
    rvx[me_r] = sv[...]

    for d in range(1, n_ch):
        q = lax.rem(me + d, n_ch)
        for k in range(chunks):
            came(rb, e_s, e_r, q, k).wait_recv()

    def unpack(q, carry):
        for k in range(chunks):
            at = q * blk + k * pair
            grad = rb[q, k, pl.ds(pair, pair), :]
            gb[pl.ds(pl.multiple_of(at, 16), pair), :] = grad
            gs[HALF, pl.ds(pl.multiple_of(HALF * cd + at, 8), pair), :] = grad.astype(F32)
        return carry

    lax.fori_loop(0, n_ch, unpack, 0)
    pack_edges(gs.at[HALF], edge2)
    halo2 = halo_copies(gb, edge2, hrow2, hedge2, hcorner2, h2_s, h2_r)
    for copy in halo2:
        copy.start()

    def add_rows(v):
        total = v[:cd]
        for i in range(1, share):
            total = total + v[i * cd : (i + 1) * cd]
        return total

    def tap_block(q, carry):
        g = gs[HALF, pl.ds(pl.multiple_of((HALF + q * share) * cd, 8), blk), :]
        for b in range(KW):
            for a in range(KW):
                x = xs[b, pl.ds(pl.multiple_of((q * share + a) * cd, 8), blk), :]
                taps[pl.ds((a * KW + b) * cd, cd), :] += add_rows(g * x)
        taps[pl.ds(KW * KW * cd, cd), :] += add_rows(g)
        return carry

    lax.fori_loop(0, n_ch // 2, tap_block, 0)

    for k in range(1, n_row):
        r = lax.rem(me_r + k, n_row)
        remote(rx.at[r], rx.at[r], x_s.at[r], x_r.at[r], row=r, col=me_c, ch=me).wait_recv()
        remote(rvx.at[r], rvx.at[r], vx_s.at[r], vx_r.at[r], row=r, col=me_c, ch=me).wait_recv()
    for q in range(0, n_ch, 2):
        at = pl.ds(q * hb, 2 * hb)
        total = rx[0, at, :].astype(F32)
        for r in range(1, n_row):
            total = total + rx[r, at, :].astype(F32)
        sy[q] = total[:hb]
        sy[q + 1] = total[hb:]
    total = rvx[0]
    for r in range(1, n_row):
        total = total + rvx[r]
    svy[...] = total

    def y_copies(k):
        q = lax.rem(me + k, n_ch)
        return (
            remote(sy.at[q], ry.at[me], y_s.at[q], y_r.at[me], row=me_r, col=me_c, ch=q),
            remote(svy, rvy.at[me], vy_s.at[q], vy_r.at[me], row=me_r, col=me_c, ch=q),
        )

    for k in range(1, n_ch):
        for copy in y_copies(k):
            copy.start()
    ry[me] = sy[me]
    rvy[me] = svy[...]

    lax.fori_loop(n_ch // 2, n_ch, tap_block, 0)
    lane_d = lane_iota(cd)

    def tap_sum(t, acc):
        col = jnp.sum(taps[pl.ds(pl.multiple_of(t * cd, 8), cd), :], axis=1, keepdims=True)
        return jnp.where(lane_d == t, col, acc)

    st[...] = lax.fori_loop(0, KW * KW + 1, tap_sum, jnp.zeros((cd, LANES), F32))

    def t_copy(k):
        r = lax.rem(me_r + k, n_row)
        return remote(st, rt.at[me_r], t_s.at[r], t_r.at[me_r], row=r, col=me_c, ch=me)

    for k in range(1, n_row):
        t_copy(k).start()
    rt[me_r] = st[...]

    for k in range(1, n_ch):
        q = lax.rem(me + k, n_ch)
        came(ry, y_s, y_r, q).wait_recv()
        came(rvy, vy_s, vy_r, q).wait_recv()
    total, vtotal = ry[0], rvy[0]
    for q in range(1, n_ch):
        total = total + ry[q]
        vtotal = vtotal + rvy[q]
    for i in range(hb // 8):
        for j in range(3):
            zt[3 * i + j] = total[8 * i : 8 * i + 8, j * LANES : (j + 1) * LANES]
    zt[n_gw] = vtotal[:, :LANES]
    zt[n_gw + 1] = vtotal[:, LANES:]
    for k in range(1, n_row):
        r = lax.rem(me_r + k, n_row)
        remote(rt.at[r], rt.at[r], t_s.at[r], t_r.at[r], row=r, col=me_c, ch=me).wait_recv()
    ttotal = rt[0]
    for r in range(1, n_row):
        ttotal = ttotal + rt[r]
    for i in range(cd // 8):
        zt[n_gw + 2 + i] = ttotal[8 * i : 8 * i + 8]

    for i in range(len(reach)):
        if i == len(reach) - 1:
            pl.semaphore_wait(ring.at[i], 2)

    def z_copy(t):
        owner = lax.rem(t, n_col)
        return remote(zt.at[t], rz.at[t, me_c], z_s.at[t], z_r.at[t, me_c], row=me_r, col=owner, ch=me)

    def z_send(t, carry):
        mine = lax.rem(t, n_col) == me_c

        @pl.when(jnp.logical_not(mine))
        def _():
            z_copy(t).start()

        @pl.when(mine)
        def _():
            rz[t, me_c] = zt[t]

        return carry

    lax.fori_loop(0, n_t, z_send, 0)

    for copy in halo2:
        copy.wait_recv()
    shifted_copies(gs, hrow2, hedge2, hcorner2)

    def backward(q, carry):
        start = cot[q].astype(F32)
        rows_q = pl.ds(pl.multiple_of(q * blk, 16), blk)
        gin[rows_q, :] = conv(gs, q * share, start, True).astype(BF16)
        for k in range(chunks):
            at = pl.ds(pl.multiple_of(q * blk + k * pair, 16), pair)
            out[at, :] = (feat[at, :].astype(F32) + rb[q, k, pl.ds(0, pair), :].astype(F32)).astype(BF16)
        return carry

    lax.fori_loop(0, n_ch, backward, 0)

    def a_copy(t, c):
        return remote(zs.at[t], zs.at[t], a_s.at[t, c], a_r.at[t], row=me_r, col=c, ch=me)

    def z_own(t, carry):
        @pl.when(lax.rem(t, n_col) == me_c)
        def _():
            def one(d, c2):
                c = lax.rem(me_c + d, n_col)
                remote(rz.at[t, c], rz.at[t, c], z_s.at[t], z_r.at[t, c], row=me_r, col=c, ch=me).wait_recv()
                return c2

            lax.fori_loop(1, n_col, one, 0)
            total = rz[t, 0]
            for c in range(1, n_col):
                total = total + rz[t, c]
            zs[t] = total

            def give(d, c2):
                a_copy(t, lax.rem(me_c + d, n_col)).start()
                return c2

            lax.fori_loop(1, n_col, give, 0)

        return carry

    lax.fori_loop(0, n_t, z_own, 0)

    def z_arrived(t, carry):
        @pl.when(lax.rem(t, n_col) != me_c)
        def _():
            a_copy(t, lax.rem(t, n_col)).wait_recv()

        return carry

    lax.fori_loop(0, n_t, z_arrived, 0)

    gw = zs.at[pl.ds(0, n_gw)]

    def f_copy(k):
        r = lax.rem(me_r + k, n_row)
        return remote(gw, gw_out.at[me_r], f_s.at[r], f_r.at[me_r], row=r, col=me_c, ch=me)

    for k in range(1, n_row):
        f_copy(k).start()
    gw_out[me_r] = zs[pl.ds(0, n_gw)]
    for j in range(2):
        v_out[:, j * LANES : (j + 1) * LANES] = zs[n_gw + j]
    for i in range(cd // 8):
        t_out[pl.ds(8 * i, 8), :] = zs[n_gw + 2 + i]

    for copy in halo1 + halo2:
        copy.wait_send()
    for k in range(1, n_ch):
        cot_copy(k).wait_send()
        q = lax.rem(me + k, n_ch)
        mix_copy(q).wait_send()
        for j in range(chunks):
            exit_copy(q, j).wait_send()
        for copy in y_copies(k):
            copy.wait_send()
    for k in range(1, n_row):
        for copy in x_copies(k):
            copy.wait_send()
        t_copy(k).wait_send()

    def z_drain(t, carry):
        mine = lax.rem(t, n_col) == me_c

        @pl.when(jnp.logical_not(mine))
        def _():
            z_copy(t).wait_send()

        @pl.when(mine)
        def _():
            def one(d, c2):
                a_copy(t, lax.rem(me_c + d, n_col)).wait_send()
                return c2

            lax.fori_loop(1, n_col, one, 0)

        return carry

    lax.fori_loop(0, n_t, z_drain, 0)
    for k in range(1, n_row):
        r = lax.rem(me_r + k, n_row)
        remote(gw_out.at[r], gw_out.at[r], f_s.at[r], f_r.at[r], row=r, col=me_c, ch=me).wait_recv()
        f_copy(k).wait_send()


def run_block(dims, feat, cot, dw_kernel, dw_bias, cols, in_bias, w_in, w_out):
    n_row, n_col, n_ch, cd, rows, chan, hid = dims
    share = rows // n_ch
    chunks = share // 2
    blk = share * cd
    hb = hid // n_ch // n_row
    n_gw = hb // 8 * 3
    n_t = n_gw + 2 + cd // 8
    pitch = -(-cd // 16) * 16
    n_tiles = rows // 32
    lanes_w = 3 * LANES
    padded = (rows + 2 * HALF) * cd
    vmem = lambda *shape: pltpu.VMEM(shape[:-1], shape[-1])
    dma = lambda *shape: pltpu.SemaphoreType.DMA(shape)
    halo_bufs = [
        vmem(2, n_tiles, pitch, LANES, BF16),
        vmem(2, 4 * cd, LANES, BF16),
        vmem(2, n_tiles, pitch, LANES, BF16),
        vmem(2, 2, pitch, LANES, BF16),
    ]
    scratch = [
        vmem(KW, padded, LANES, F32),
        vmem(KW, padded, LANES, F32),
        vmem(KW * KW * cd, LANES, F32),
        vmem(cd, LANES, F32),
        vmem(4, chan, LANES, F32),
        *halo_bufs,
        *halo_bufs,
        vmem(2, n_tiles + 2, cd, LANES, F32),
        vmem(rows * cd, LANES, BF16),
        vmem(n_ch, blk, LANES, BF16),
        vmem(n_ch, blk, LANES, BF16),
        vmem(n_ch, blk, LANES, BF16),
        vmem(n_ch, chunks, 4 * cd, LANES, BF16),
        vmem(n_ch, chunks, 4 * cd, LANES, BF16),
        vmem(chan + 64, hid, BF16),
        vmem(hid, chan + 64, BF16),
        vmem(chan, hid, BF16),
        vmem(hid, chan + 64, F32),
        vmem(hid, chan, F32),
        vmem(4, chan, LANES, F32),
        vmem(n_row, n_ch * hb, lanes_w, BF16),
        vmem(n_row, n_ch * hb, lanes_w, BF16),
        vmem(8, 2 * LANES, F32),
        vmem(n_row, 8, 2 * LANES, F32),
        vmem(n_ch, hb, lanes_w, F32),
        vmem(n_ch, hb, lanes_w, F32),
        vmem(8, 2 * LANES, F32),
        vmem(n_ch, 8, 2 * LANES, F32),
        vmem((KW * KW + 1) * cd, LANES, F32),
        vmem(cd, LANES, F32),
        vmem(n_row, cd, LANES, F32),
        vmem(n_t, 8, LANES, F32),
        vmem(n_t, n_col, 8, LANES, F32),
        vmem(n_t, 8, LANES, F32),
        dma(8), dma(8),
        dma(8), dma(8),
        dma(n_ch), dma(n_ch),
        dma(n_ch), dma(n_ch),
        dma(n_ch, chunks), dma(n_ch, chunks),
        dma(n_row), dma(n_row),
        dma(n_row), dma(n_row),
        dma(n_ch), dma(n_ch),
        dma(n_ch), dma(n_ch),
        dma(n_row), dma(n_row),
        dma(n_t), dma(n_t, n_col),
        dma(n_t, n_col), dma(n_t),
        dma(n_row), dma(n_row),
        pltpu.SemaphoreType.REGULAR((4,)),
    ]
    whole = pl.BlockSpec(memory_space=pltpu.VMEM)
    return pl.pallas_call(
        functools.partial(block_kernel, dims),
        name="convnext_block",
        out_shape=(
            jax.ShapeDtypeStruct((rows * cd, LANES), BF16),
            jax.ShapeDtypeStruct((rows * cd, LANES), BF16),
            jax.ShapeDtypeStruct((n_row, n_gw, 8, LANES), F32),
            jax.ShapeDtypeStruct((8, 2 * LANES), F32),
            jax.ShapeDtypeStruct((cd, LANES), F32),
        ),
        in_specs=[whole] * 8,
        out_specs=(whole,) * 5,
        scratch_shapes=scratch,
        compiler_params=pltpu.CompilerParams(
            collective_id=0, has_side_effects=True, vmem_limit_bytes=56 * 1024 * 1024
        ),
    )(feat, cot, dw_kernel, dw_bias, cols, in_bias, w_in, w_out)


def body(
    n_row,
    n_col,
    n_ch,
    features,
    cotangent,
    dw_kernel,
    dw_bias,
    ln_gain,
    ln_bias,
    w_in,
    in_bias,
    w_out,
    out_bias,
    layer_scale,
):
    cd, rows, wide = features.shape
    chan, hid = w_in.shape
    dims = (n_row, n_col, n_ch, cd, rows, chan, hid)
    feat = features.transpose(1, 0, 2).reshape(rows * cd, wide)
    cot = cotangent.transpose(1, 0, 2).reshape(n_ch, rows // n_ch * cd, wide)
    cols = jnp.stack([ln_gain, ln_bias, out_bias, layer_scale], axis=1)
    out, gin, gw, vecs, taps = run_block(
        dims, feat, cot, dw_kernel, dw_bias[:, None], cols, in_bias[None], w_in, w_out
    )
    back = lambda v: v.reshape(rows, cd, wide).transpose(1, 0, 2)
    factor = 1.0 / math.sqrt(rows * n_row * wide * n_col)
    hs = hid // n_ch
    gw = gw.reshape(n_row, hs // n_row // 8, 3, 8, LANES).transpose(0, 1, 3, 2, 4).reshape(hs, 3 * LANES)
    gw = gw * factor
    rest = chan - LANES
    g_in = jnp.concatenate([gw[:, :LANES], gw[:, 2 * LANES : 2 * LANES + rest]], axis=1).T
    g_out = jnp.concatenate([gw[:, LANES : 2 * LANES], gw[:, 2 * LANES + 64 : 2 * LANES + 64 + rest]], axis=1)
    vecs = vecs[:, :chan] * factor
    bias = lax.dynamic_slice_in_dim(vecs[4:].reshape(-1), lax.axis_index("ch") * hs, hs, 0)
    return (
        back(out),
        back(gin),
        g_in,
        g_out,
        bias,
        vecs[:4],
        taps[:, : KW * KW + 1] * factor,
    )


def solution(mesh):
    ch = P("ch", "row", "col")
    in_specs = (ch, ch, P("ch", None), P("ch")) + (P(),) * 7
    out_specs = (ch, ch, P(None, "ch"), P("ch", None), P("ch"), P(), P("ch", None))
    sizes = (mesh.shape["row"], mesh.shape["col"], mesh.shape["ch"])
    return jax.shard_map(
        functools.partial(body, *sizes), mesh=mesh, in_specs=in_specs, out_specs=out_specs, check_vma=False
    )
```

profile of v0, /device:TPU:6, one launch (start us, length us, event | category | flops | bytes accessed | tf_op | source)
XLA Modules:
  0.0 111.3 jit_solution(131627436381450478)
XLA Ops:
  0.6 0.0 copy-start
  0.6 2.0 %copy.36 = bf16[64,24,128]{2,1,0:T(8,128)(2,1)} copy(bf16[64,24,128]{2,0,1:T(8,128)(2,1)} %bitcast.26) | data formatting | bytes 786432 | tf_op jit(solution)/shard_map/transpose | solution.py:794
  2.7 0.0 copy-done
  2.7 1.0 copy.37
  3.7 0.0 copy-done.3
  3.7 0.0 copy-start.8
  3.7 0.9 copy.40.w_out
  4.6 0.0 copy-done.8
  4.6 0.0 copy-done.9
  4.6 0.0 copy-done.10
  4.7 0.7 copy-done.7
  5.3 0.8 copy.39.cols
  6.1 0.7 copy-done.11
  6.8 0.7 copy.38.dw_bias
  7.4 0.0 copy-done.6
  7.4 0.6 broadcast_in_dim.7.in_bias
  8.0 97.2 %convnext_block.1 = (bf16[1536,128]{1,0:T(8,128)(2,1)}, bf16[1536,128]{1,0:T(8,128)(2,1)}, f32[4,9,8,128]{3,2,1,0:T(8,128)}, f32[8,256]{1,0:T(8,128)}, f32[24,128]{1,0:T(8,128)}) custom-call(bf16[1536,128]{1,0:T(8,128)(2,1)} %bitcast.22, bf16[8,192,128]{2,1,0:T(8,128)(2,1)} %bitcast.23, f32[24,49]{1,0:T(8,128)} %dw_kernel.1, f32[24,1]{1,0:T(8,128)} %copy.38.dw_bias, ...), custom_call_target="tpu_custom_call" | custom-call | tf_op jit(solution)/shard_map/convnext_block/pallas_call | solution.py:756
  105.2 0.9 broadcast_multiply_fusion
  106.2 0.0 copy-start.1
  106.2 0.0 copy-start.2
  106.2 0.1 fusion.1
  106.3 0.7 maximum_bitcast_fusion
  106.9 0.7 copy.43
  107.7 0.7 copy-done.5
  108.4 0.6 fusion.2
  109.0 0.1 reshape.39
  109.0 0.6 dynamic_slice.3
  109.6 0.0 copy-done.1
  109.6 0.0 copy-done.2
  109.6 1.1 copy_bitcast_fusion
  110.7 0.0 copy-done.4
  110.7 0.6 slice_multiply_fusion
  (11 shorter events, 0.0 us)
Async XLA Ops:
  0.6 2.1 %copy-start = (bf16[24,64,128]{2,1,0:T(8,128)(2,1)S(1)}, bf16[24,64,128]{2,1,0:T(8,128)(2,1)}, u32[]{:S(2)}) copy-start(bf16[24,64,128]{2,1,0:T(8,128)(2,1)} %param.12) | copy-start | bytes 1179652
  2.7 1.0 copy-start.3
  3.7 0.9 copy-start.8
  3.7 0.9 copy-start.9
  3.7 0.9 copy-start.10
  4.6 0.7 copy-start.7
  6.1 0.7 copy-start.11
  6.8 0.7 copy-start.6
  106.2 3.5 %copy-start.1 = (bf16[1536,128]{1,0:T(8,128)(2,1)S(1)}, bf16[1536,128]{1,0:T(8,128)(2,1)}, u32[]{:S(2)}) copy-start(bf16[1536,128]{1,0:T(8,128)(2,1)} %get-tuple-element.12) | copy-start | bytes 1179652
  106.2 3.5 %copy-start.2 = (bf16[1536,128]{1,0:T(8,128)(2,1)S(1)}, bf16[1536,128]{1,0:T(8,128)(2,1)}, u32[]{:S(2)}) copy-start(bf16[1536,128]{1,0:T(8,128)(2,1)} %get-tuple-element.13) | copy-start | bytes 1179652
  107.7 0.7 copy-start.5
  109.6 1.1 copy-start.4
where the time goes:
time: 112 us; the launch traced here: 111 us
  Pallas kernels  97.2 us (87%)
  local copies, waits for them, and re-layouts  11.2 us (10%)
  other arithmetic  2.2 us (2%)
    pallas_call x1, Pallas kernels, run_block(): pl.pallas_call(functools.partial(block_kernel, dims), name='convnext_bloc...  97.2 us
    unnamed x26, local copies, waits for them, and re-layouts  3.72 us

commit v1 on v0

v1 whole, which is shorter than its diff:
```python
import functools
import math

import jax
import jax.numpy as jnp
from jax import lax
from jax.experimental import pallas as pl
from jax.experimental.pallas import tpu as pltpu
from jax.sharding import PartitionSpec as P

KW = 7
HALF = 3
LANES = 128
SQRT_HALF = 0.7071067811865476
INV_SQRT_TWO_PI = 0.3989422804014327
EPSILON = 1e-06
MESH = pl.DeviceIdType.MESH
F32 = jnp.float32
BF16 = jnp.bfloat16

ERF_P = 0.3275911 * SQRT_HALF
ERF_A = (0.254829592, -0.284496736, 1.421413741, -1.453152027, 1.061405429)


def gelu_parts(v):
    bell = jnp.exp2((-0.5 * math.log2(math.e)) * (v * v))
    t = 1.0 / (1.0 + ERF_P * jnp.abs(v))
    poly = 0.5 * ERF_A[4]
    for a in ERF_A[3::-1]:
        poly = poly * t + 0.5 * a
    tail = poly * t * bell
    cumul = jnp.where(v >= 0, 1.0 - tail, tail)
    return v * cumul, cumul + v * (INV_SQRT_TWO_PI * bell)


def dot(a, b):
    return jnp.dot(a, b, preferred_element_type=F32)


def dot_nt(a, b):
    return lax.dot_general(a, b, (((1,), (1,)), ((), ())), preferred_element_type=F32)


def lane_iota(rows):
    return lax.broadcasted_iota(jnp.int32, (rows, LANES), 1)


def remote(src, dst, send, recv, **where):
    return pltpu.make_async_remote_copy(
        src_ref=src, dst_ref=dst, send_sem=send, recv_sem=recv, device_id=where, device_id_type=MESH
    )


def block_kernel(
    dims,
    feat,
    cot,
    dw_kernel,
    dw_bias,
    ln_gain,
    ln_bias,
    out_bias,
    layer_scale,
    in_bias,
    w_in,
    woutt,
    out,
    gin,
    fx,
    v_out,
    plain,
    ca,
    ends,
    ends2,
    xs,
    gs,
    cbuf,
    wb,
    cb,
    vecs,
    edge,
    hrow,
    hedge,
    hcorner,
    edge2,
    hrow2,
    hedge2,
    hcorner2,
    stage,
    mb,
    rm,
    rc,
    sb,
    rb,
    wa,
    wint,
    w_out,
    g1,
    g2,
    va,
    sc,
    rxc,
    sx,
    rx,
    sv,
    rvc,
    svx,
    rvx,
    sy,
    ry,
    svy,
    rvy,
    taps,
    zt,
    rz,
    zs,
    h_s,
    h_r,
    h2_s,
    h2_r,
    c_s,
    c_r,
    m_s,
    m_r,
    e_s,
    e_r,
    p_s,
    p_r,
    x_s,
    x_r,
    vx_s,
    vx_r,
    y_s,
    y_r,
    vy_s,
    vy_r,
    z_s,
    z_r,
    a_s,
    a_r,
    f_s,
    f_r,
    ring,
):
    n_row, n_col, n_ch, cd, rows, chan, hid = dims
    share = rows // n_ch
    chunks = share // 2
    blk = share * cd
    pair = 2 * cd
    hb = hid // n_ch // n_row
    n_gw = hb // 8 * 3
    n_t = n_gw + 2 + cd // 8
    kb = min(256, hid)
    n_y = n_ch // 2
    me_r = lax.axis_index("row")
    me_c = lax.axis_index("col")
    me = lax.axis_index("ch")
    core, me_y = lax.rem(me, 2), lax.div(me, 2)
    mate = me + 1 - 2 * core
    up, down = lax.rem(me_r + n_row - 1, n_row), lax.rem(me_r + 1, n_row)
    left, right = lax.rem(me_c + n_col - 1, n_col), lax.rem(me_c + 1, n_col)

    barrier = pltpu.get_barrier_semaphore()
    near = []
    for k in range(1, n_ch):
        near.append(dict(row=me_r, col=me_c, ch=lax.rem(me + k, n_ch)))
    for k in range(1, n_row):
        near.append(dict(row=lax.rem(me_r + k, n_row), col=me_c, ch=me))
    for c in (left, right):
        for r in (me_r, up, down):
            near.append(dict(row=r, col=c, ch=me))
    for where in near:
        pl.semaphore_signal(barrier, inc=1, device_id=where, device_id_type=MESH)

    edge_pitch = edge.shape[2]
    n_tiles = rows // 32

    def pack_edges(src, buf, row_ends):
        lane = lane_iota(cd)
        acc = [jnp.zeros((cd, LANES), F32)] * (2 * n_tiles)
        for t in range(32):
            keep = (lane >= 4 * t) & (lane < 4 * t + 4)
            for k in range(n_tiles):
                x = src[pl.ds((HALF + 32 * k + t) * cd, cd), :]
                for side, turn in ((0, 4 * t), (1, (4 * t + 4) % LANES)):
                    moved = pltpu.roll(x, turn, 1) if turn else x
                    acc[2 * k + side] = jnp.where(keep, moved, acc[2 * k + side])
        pad = jnp.zeros((edge_pitch - cd, LANES), F32)
        for k in range(n_tiles):
            for side in range(2):
                full = acc[2 * k + side]
                if edge_pitch > cd:
                    full = jnp.concatenate([full, pad], axis=0)
                buf[side, k] = full.astype(BF16)
        row_ends[0] = src[pl.ds(HALF * cd, 4 * cd), :].astype(BF16)
        row_ends[1] = src[pl.ds((HALF + rows - 4) * cd, 4 * cd), :].astype(BF16)

    def by_rows(src):
        for c in range(cd):
            plain[pl.ds(c * rows, rows), :] = src[c].astype(F32)

    def plain_row(i):
        return plain[pl.ds(i, cd, stride=rows), :]

    by_rows(feat)
    for i in range(rows):
        xs[HALF, pl.ds((HALF + i) * cd, cd), :] = plain_row(i)
    pack_edges(xs.at[HALF], edge, ends)

    pl.semaphore_wait(barrier, len(near))

    def halo_copies(src, ebuf, rbuf, lbuf, cbuf, ss, rs):
        copies = [
            remote(src.at[0], rbuf.at[1], ss.at[0], rs.at[0], row=up, col=me_c, ch=me),
            remote(src.at[1], rbuf.at[0], ss.at[1], rs.at[1], row=down, col=me_c, ch=me),
            remote(ebuf.at[0], lbuf.at[1], ss.at[2], rs.at[2], row=me_r, col=left, ch=me),
            remote(ebuf.at[1], lbuf.at[0], ss.at[3], rs.at[3], row=me_r, col=right, ch=me),
        ]
        copies.append(remote(ebuf.at[0, 0], cbuf.at[1, 1], ss.at[4], rs.at[4], row=up, col=left, ch=me))
        copies.append(remote(ebuf.at[1, 0], cbuf.at[1, 0], ss.at[5], rs.at[5], row=up, col=right, ch=me))
        copies.append(
            remote(ebuf.at[0, n_tiles - 1], cbuf.at[0, 1], ss.at[6], rs.at[6], row=down, col=left, ch=me)
        )
        copies.append(
            remote(ebuf.at[1, n_tiles - 1], cbuf.at[0, 0], ss.at[7], rs.at[7], row=down, col=right, ch=me)
        )
        return copies

    halo1 = halo_copies(ends, edge, hrow, hedge, hcorner, h_s, h_r)
    for copy in halo1:
        copy.start()

    def cot_copy(k):
        q = lax.rem(me + k, n_ch)
        return remote(ca.at[q], rc.at[me], c_s.at[q], c_r.at[me], row=me_r, col=me_c, ch=q)

    def came(buf, ss, rs, q, idx=None):
        dst = buf.at[q] if idx is None else buf.at[q, idx]
        recv = rs.at[q] if idx is None else rs.at[q, idx]
        send = ss.at[q] if idx is None else ss.at[q, idx]
        return remote(dst, dst, send, recv, row=me_r, col=me_c, ch=q)

    by_rows(cot)
    for i in range(0, rows, 2):
        ca[i // share, pl.ds(i % share * cd, pair), :] = jnp.concatenate(
            [plain_row(i), plain_row(i + 1)], axis=0
        ).astype(BF16)
    for k in range(1, n_ch):
        cot_copy(k).start()

    for t in range(KW * KW):
        wb[pl.ds(t * cd, cd), :] = jnp.broadcast_to(dw_kernel[:, t : t + 1], (cd, LANES))

    def as_row(ref, width):
        row = ref[...].reshape(1, ref.shape[0])
        if width > ref.shape[0]:
            row = jnp.concatenate([row, jnp.zeros((1, width - ref.shape[0]), F32)], axis=1)
        return row

    wide_rows = [as_row(v, 2 * LANES) for v in (ln_gain, ln_bias, out_bias, layer_scale, dw_bias)]
    table = jnp.concatenate(wide_rows + [jnp.zeros((LANES - 5, 2 * LANES), F32)], axis=0).T
    for k in range(4):
        vecs[k] = jnp.broadcast_to(table[:chan, k : k + 1], (chan, LANES))
    cb[...] = jnp.broadcast_to(table[:cd, 4:5], (cd, LANES))
    eye = lambda n: (
        lax.broadcasted_iota(jnp.int32, (n, n), 0) == lax.broadcasted_iota(jnp.int32, (n, n), 1)
    ).astype(BF16)
    wa[pl.ds(0, chan), :] = w_in[...]
    bias_row = as_row(in_bias, hid)
    hi = bias_row.astype(BF16).astype(F32)
    lo = bias_row - hi
    row_id = lax.broadcasted_iota(jnp.int32, (64, hid), 0)
    wa[pl.ds(chan, 64), :] = jnp.where(
        row_id == 0, jnp.broadcast_to(hi, (64, hid)), jnp.where(row_id == 1, jnp.broadcast_to(lo, (64, hid)), 0.0)
    ).astype(BF16)
    for k in range(hid // kb):
        wint[pl.ds(k * kb, kb), :] = dot_nt(eye(kb), wa[:, k * kb : (k + 1) * kb]).astype(BF16)
        w_out[pl.ds(k * kb, kb), :] = dot_nt(eye(kb), woutt[:, k * kb : (k + 1) * kb]).astype(BF16)
    g1[...] = jnp.zeros_like(g1)
    g2[...] = jnp.zeros_like(g2)
    va[...] = jnp.zeros_like(va)
    taps[...] = jnp.zeros_like(taps)
    rc[me] = ca[me]

    def as_f32(flag):
        return jnp.where(flag, 1.0, 0.0).astype(F32)

    def shifted_copies(buf, rbuf, lbuf, cbuf):
        has_up, has_down = as_f32(me_r > 0), as_f32(me_r < n_row - 1)
        has_left, has_right = as_f32(me_c > 0), as_f32(me_c < n_col - 1)
        buf[HALF, pl.ds(0, HALF * cd), :] = rbuf[0].astype(F32)[cd:] * has_up
        buf[HALF, pl.ds((HALF + rows) * cd, HALF * cd), :] = rbuf[1].astype(F32)[: HALF * cd] * has_down
        for side, has in ((0, has_left), (1, has_right)):
            stage[side, 0] = cbuf[0, side].astype(F32)[:cd] * (has * has_up)
            for k in range(n_tiles):
                stage[side, 1 + k] = lbuf[side, k].astype(F32)[:cd] * has
            stage[side, 1 + n_tiles] = cbuf[1, side].astype(F32)[:cd] * (has * has_down)
        lane = lane_iota(cd)

        total = rows + 2 * HALF
        step = next(u for u in (7, 5, 2, 1) if total % u == 0)

        def some_rows(j, carry):
            held = []
            for u in range(step):
                i = j * step + u
                at = i + 32 - HALF
                tile, t = lax.div(at, 32), lax.rem(at, 32)
                where = pl.ds(pl.multiple_of(i * cd, 8), cd)
                held.append((where, t, stage[1, tile], stage[0, tile], buf[HALF, where, :]))
            for where, t, from_right, from_left, x in held:
                halo = jnp.where(
                    lane < 64,
                    pltpu.roll(from_right, lax.rem(LANES - 4 * t, LANES), 1),
                    pltpu.roll(from_left, 124 - 4 * t, 1),
                )
                for s in range(1, HALF + 1):
                    buf[HALF + s, where, :] = pltpu.roll(jnp.where(lane < s, halo, x), LANES - s, 1)
                    buf[HALF - s, where, :] = pltpu.roll(jnp.where(lane >= LANES - s, halo, x), s, 1)
            return carry

        lax.fori_loop(0, total // step, some_rows, 0)

    for copy in halo1:
        copy.wait_recv()

    reach = []
    r = 2
    while r < n_col // 2:
        reach.append(r)
        r *= 2

    def tell(i):
        for step in (reach[i], n_col - reach[i]):
            pl.semaphore_signal(
                ring.at[i],
                inc=1,
                device_id=dict(row=me_r, col=lax.rem(me_c + step, n_col), ch=me),
                device_id_type=MESH,
            )

    if reach:
        tell(0)

    shifted_copies(xs, hrow, hedge, hcorner)

    def conv(buf, base, start, flip):
        def group(g, carry):
            acc = [cb[pl.ds(pl.multiple_of(8 * g, 8), 8), :] if start else jnp.zeros((8, LANES), F32)] * share
            for b in range(KW):
                x = [
                    buf[b, pl.ds(pl.multiple_of((base + i) * cd + 8 * g, 8), 8), :]
                    for i in range(share + 2 * HALF)
                ]
                for a in range(KW):
                    tap = (KW - 1 - a) * KW + KW - 1 - b if flip else a * KW + b
                    w = wb[pl.ds(pl.multiple_of(tap * cd + 8 * g, 8), 8), :]
                    for r in range(share):
                        acc[r] = acc[r] + w * x[r + a]
            for r in range(share):
                cbuf[pl.ds(pl.multiple_of(r * cd + 8 * g, 8), 8), :] = acc[r]
            return carry

        lax.fori_loop(0, cd // 8, group, 0)
        return cbuf[...]

    def mix_copy(q):
        return remote(mb.at[q], rm.at[me], m_s.at[q], m_r.at[me], row=me_r, col=me_c, ch=q)

    def forward(k, carry):
        q = lax.rem(me + 1 + k, n_ch)
        mb[q] = conv(xs, q * share, True, False).astype(BF16)

        @pl.when(k < n_ch - 1)
        def _():
            mix_copy(q).start()

        return carry

    lax.fori_loop(0, n_ch, forward, 0)
    rm[me] = mb[me]

    for k in range(1, n_ch):
        q = lax.rem(me + k, n_ch)
        came(rc, c_s, c_r, q).wait_recv()
        came(rm, m_s, m_r, q).wait_recv()

    if len(reach) > 1:
        pl.semaphore_wait(ring.at[0], 2)
        tell(1)

    px = 2 * LANES
    ones_rows = (lax.broadcasted_iota(jnp.int32, (64, px), 0) < 2).astype(F32).astype(BF16)

    def wide(v):
        return jnp.concatenate([v, v], axis=1)

    def gather(buf, at):
        parts = []
        for q in range(n_ch):
            both = buf[q, at, :].astype(F32)
            parts.append(jnp.concatenate([both[:cd], both[cd:]], axis=1))
        return jnp.concatenate(parts, axis=0)

    def exit_copy(q, k):
        return remote(sb.at[q, k], rb.at[me, k], e_s.at[q, k], e_r.at[me, k], row=me_r, col=me_c, ch=q)

    def fold(v):
        return v[:, :LANES] + v[:, LANES:]

    def chunk(k, carry):
        at = pl.ds(pl.multiple_of(k * pair, 16), pair)
        gain, shift, outb, scale = (wide(vecs[i]) for i in range(4))
        values = gather(rm, at)
        centre = jnp.mean(values, axis=0, keepdims=True)
        away = values - centre
        inv_std = lax.rsqrt(jnp.mean(away * away, axis=0, keepdims=True) + EPSILON)
        normed = away * inv_std
        scaled = (normed * gain + shift).astype(BF16)
        scaled = jnp.concatenate([scaled, ones_rows], axis=0)
        cotan = gather(rc, at)
        cots = (cotan * scale).astype(BF16)
        projected = jnp.zeros((chan, px), F32)
        grad_scaled = jnp.zeros((chan, px), F32)
        for j in range(hid // kb):
            rows_j = pl.ds(j * kb, kb)
            act, slope = gelu_parts(dot(wint[rows_j, :], scaled))
            hidden = act.astype(BF16)
            grad_hidden = (dot(w_out[rows_j, :], cots) * slope).astype(BF16)
            projected = projected + dot(woutt[:, j * kb : (j + 1) * kb], hidden)
            grad_scaled = grad_scaled + dot(w_in[:, j * kb : (j + 1) * kb], grad_hidden)
            g1[rows_j, :] += dot_nt(grad_hidden, scaled)
            g2[rows_j, :] += dot_nt(hidden, cots)
        projected = projected + outb
        branch = scale * projected
        va[0] += fold(cots.astype(F32))
        va[1] += fold(grad_scaled * normed)
        va[2] += fold(grad_scaled)
        va[3] += fold(cotan * projected)
        gn = grad_scaled * gain
        m1 = jnp.mean(gn, axis=0, keepdims=True)
        m2 = jnp.mean(gn * normed, axis=0, keepdims=True)
        gm = (gn - m1 - normed * m2) * inv_std
        for q in range(n_ch):
            for i, v in enumerate((branch, gm)):
                piece = v[q * cd : (q + 1) * cd]
                sb[q, k, pl.ds(i * pair, pair), :] = jnp.concatenate(
                    [piece[:, :LANES], piece[:, LANES:]], axis=0
                ).astype(BF16)
        for d in range(1, n_ch):
            exit_copy(lax.rem(me + d, n_ch), k).start()
        rb[me, k] = sb[me, k]
        return carry

    lax.fori_loop(0, chunks, chunk, 0)

    pair_rows = 2 * hb
    half = lane_iota(pair_rows) < 64
    for par in range(2):
        for r in range(n_row):
            for y in range(0, n_y, 2):
                at = [(2 * (y + i) + par) * hb * n_row + r * hb for i in range(min(2, n_y))]
                a, b = (jnp.concatenate([g[pl.ds(at_i, hb), :] for at_i in at], axis=0) for g in (g1, g2))
                size = hb * len(at)
                b_hi = pltpu.roll(
                    jnp.concatenate([b[:, LANES:], jnp.zeros((size, 2 * LANES - chan), F32)], axis=1), 64, 1
                )
                sc[par, r, pl.ds(y * hb, size), :] = jnp.concatenate(
                    [a[:, :LANES], b[:, :LANES], jnp.where(half[:size], a[:, LANES:], b_hi)], axis=1
                ).astype(BF16)
    p_copy = remote(sc.at[1 - core], rxc, p_s.at[0], p_r.at[0], row=me_r, col=me_c, ch=mate)
    p_copy.start()
    lane_c = lane_iota(chan)
    table = jnp.zeros((chan, LANES), F32)
    for i in range(4):
        table = jnp.where(lane_c == i, jnp.sum(va[i], axis=1, keepdims=True), table)
    for i in range(hid // chan):
        part = pltpu.roll(g1[pl.ds(i * chan, chan), LANES:], LANES - 64 + 4 + i, 1)
        table = jnp.where(lane_c == 4 + i, part, table)
    table = jnp.concatenate([table, jnp.zeros((2 * LANES - chan, LANES), F32)], axis=0)
    sv[...] = table.T[:8]
    pv_copy = remote(sv, rvc, p_s.at[1], p_r.at[1], row=me_r, col=me_c, ch=mate)
    pv_copy.start()

    def x_copies(k):
        r = lax.rem(me_r + k, n_row)
        return (
            remote(sx.at[r], rx.at[me_r], x_s.at[r], x_r.at[me_r], row=r, col=me_c, ch=me),
            remote(svx, rvx.at[me_r], vx_s.at[r], vx_r.at[me_r], row=r, col=me_c, ch=me),
        )

    p_copy.wait_recv()
    pv_copy.wait_recv()
    for r in range(n_row):
        sx[r] = (sc[core, r].astype(F32) + rxc[r].astype(F32)).astype(BF16)
    svx[...] = sv[...] + rvc[...]
    for k in range(1, n_row):
        for copy in x_copies(k):
            copy.start()
    rx[me_r] = sx[me_r]
    rvx[me_r] = svx[...]

    for d in range(1, n_ch):
        q = lax.rem(me + d, n_ch)
        for k in range(chunks):
            came(rb, e_s, e_r, q, k).wait_recv()

    def unpack(q, carry):
        for k in range(chunks):
            at = q * blk + k * pair
            gs[HALF, pl.ds(pl.multiple_of(HALF * cd + at, 8), pair), :] = rb[q, k, pl.ds(pair, pair), :].astype(F32)
        return carry

    lax.fori_loop(0, n_ch, unpack, 0)
    pack_edges(gs.at[HALF], edge2, ends2)
    halo2 = halo_copies(ends2, edge2, hrow2, hedge2, hcorner2, h2_s, h2_r)
    for copy in halo2:
        copy.start()

    def tap_block(q, carry):
        def group(g, c2):
            grad = [
                gs[HALF, pl.ds(pl.multiple_of((HALF + q * share + r) * cd + 8 * g, 8), 8), :]
                for r in range(share)
            ]

            def add(tap, terms):
                while len(terms) > 1:
                    terms = [sum(terms[i : i + 2]) for i in range(0, len(terms), 2)]
                taps[pl.ds(pl.multiple_of(tap * cd + 8 * g, 8), 8), :] += terms[0]

            for b in range(KW):
                x = [
                    xs[b, pl.ds(pl.multiple_of((q * share + i) * cd + 8 * g, 8), 8), :]
                    for i in range(share + 2 * HALF)
                ]
                for a in range(KW):
                    add(a * KW + b, [grad[r] * x[r + a] for r in range(share)])
            add(KW * KW, grad)
            return c2

        return lax.fori_loop(0, cd // 8, group, carry)

    lax.fori_loop(0, n_ch // 2, tap_block, 0)

    for k in range(1, n_row):
        r = lax.rem(me_r + k, n_row)
        remote(rx.at[r], rx.at[r], x_s.at[r], x_r.at[r], row=r, col=me_c, ch=me).wait_recv()
        remote(rvx.at[r], rvx.at[r], vx_s.at[r], vx_r.at[r], row=r, col=me_c, ch=me).wait_recv()
    total, vtotal = rx[0].astype(F32), rvx[0]
    for r in range(1, n_row):
        total = total + rx[r].astype(F32)
        vtotal = vtotal + rvx[r]
    for y in range(n_y):
        sy[y] = total[y * hb : (y + 1) * hb]
    svy[...] = vtotal

    def y_copies(k):
        y = lax.rem(me_y + k, n_y)
        q = 2 * y + core
        return (
            remote(sy.at[y], ry.at[me_y], y_s.at[y], y_r.at[me_y], row=me_r, col=me_c, ch=q),
            remote(svy, rvy.at[me_y], vy_s.at[y], vy_r.at[me_y], row=me_r, col=me_c, ch=q),
        )

    for k in range(1, n_y):
        for copy in y_copies(k):
            copy.start()
    ry[me_y] = sy[me_y]
    rvy[me_y] = svy[...]

    lax.fori_loop(n_ch // 2, n_ch, tap_block, 0)
    lane_d = lane_iota(cd)
    tap_table = jnp.zeros((cd, LANES), F32)
    for t in range(KW * KW + 1):
        col = jnp.sum(taps[pl.ds(t * cd, cd), :], axis=1, keepdims=True)
        tap_table = jnp.where(lane_d == t, col, tap_table)
    for i in range(cd // 8):
        zt[n_gw + 2 + i] = tap_table[8 * i : 8 * i + 8]

    for k in range(1, n_y):
        y = lax.rem(me_y + k, n_y)
        q = 2 * y + core
        remote(ry.at[y], ry.at[y], y_s.at[y], y_r.at[y], row=me_r, col=me_c, ch=q).wait_recv()
        remote(rvy.at[y], rvy.at[y], vy_s.at[y], vy_r.at[y], row=me_r, col=me_c, ch=q).wait_recv()
    total, vtotal = ry[0], rvy[0]
    for y in range(1, n_y):
        total = total + ry[y]
        vtotal = vtotal + rvy[y]
    for i in range(hb // 8):
        for j in range(3):
            zt[3 * i + j] = total[8 * i : 8 * i + 8, j * LANES : (j + 1) * LANES]
    zt[n_gw] = vtotal[:, :LANES]
    zt[n_gw + 1] = vtotal[:, LANES:]

    for i in range(len(reach)):
        if i == len(reach) - 1:
            pl.semaphore_wait(ring.at[i], 2)

    def z_copy(t):
        owner = lax.rem(t, n_col)
        return remote(zt.at[t], rz.at[t, me_c], z_s.at[t], z_r.at[t, me_c], row=me_r, col=owner, ch=me)

    def z_send(t, carry):
        mine = lax.rem(t, n_col) == me_c

        @pl.when(jnp.logical_not(mine))
        def _():
            z_copy(t).start()

        @pl.when(mine)
        def _():
            rz[t, me_c] = zt[t]

        return carry

    lax.fori_loop(0, n_t, z_send, 0)

    for copy in halo2:
        copy.wait_recv()
    shifted_copies(gs, hrow2, hedge2, hcorner2)

    def backward(q, carry):
        rows_q = pl.ds(pl.multiple_of(q * blk, 16), blk)
        gin[rows_q, :] = (conv(gs, q * share, False, True) + ca[q].astype(F32)).astype(BF16)
        for k in range(chunks):
            at = pl.ds(pl.multiple_of(q * blk + k * pair, 16), pair)
            here = xs[HALF, pl.ds(pl.multiple_of(HALF * cd + q * blk + k * pair, 8), pair), :]
            out[at, :] = (here + rb[q, k, pl.ds(0, pair), :].astype(F32)).astype(BF16)
        return carry

    lax.fori_loop(0, n_ch, backward, 0)

    def a_copy(t, c):
        return remote(zs.at[t], zs.at[t], a_s.at[t, c], a_r.at[t], row=me_r, col=c, ch=me)

    def z_own(t, carry):
        @pl.when(lax.rem(t, n_col) == me_c)
        def _():
            def one(d, c2):
                c = lax.rem(me_c + d, n_col)
                remote(rz.at[t, c], rz.at[t, c], z_s.at[t], z_r.at[t, c], row=me_r, col=c, ch=me).wait_recv()
                return c2

            lax.fori_loop(1, n_col, one, 0)
            total = rz[t, 0]
            for c in range(1, n_col):
                total = total + rz[t, c]
            zs[t] = total

            def give(d, c2):
                a_copy(t, lax.rem(me_c + d, n_col)).start()
                return c2

            lax.fori_loop(1, n_col, give, 0)

        return carry

    lax.fori_loop(0, n_t, z_own, 0)

    def f_copy(t, k):
        slot = jnp.where(t < n_gw, t, t - 2)
        r = lax.rem(me_r + k, n_row)
        return remote(zs.at[t], fx.at[me_r, slot], f_s.at[t, r], f_r.at[me_r, t], row=r, col=me_c, ch=me)

    def goes_on(t):
        return (t < n_gw) | (t >= n_gw + 2)

    def hand_on(t):
        @pl.when(goes_on(t))
        def _():
            for k in range(1, n_row):
                f_copy(t, k).start()

    def z_arrived(i, carry):
        t = i

        @pl.when(lax.rem(t, n_col) != me_c)
        def _():
            a_copy(t, lax.rem(t, n_col)).wait_recv()

        hand_on(t)
        return carry

    lax.fori_loop(0, n_t, z_arrived, 0)
    fx[me_r, pl.ds(0, n_gw)] = zs[pl.ds(0, n_gw)]
    fx[me_r, pl.ds(n_gw, cd // 8)] = zs[pl.ds(n_gw + 2, cd // 8)]
    v_out[...] = zs[pl.ds(n_gw, 2)]

    for copy in halo1 + halo2:
        copy.wait_send()
    for k in range(1, n_ch):
        cot_copy(k).wait_send()
        q = lax.rem(me + k, n_ch)
        mix_copy(q).wait_send()
        for j in range(chunks):
            exit_copy(q, j).wait_send()
    p_copy.wait_send()
    pv_copy.wait_send()
    for k in range(1, n_y):
        for copy in y_copies(k):
            copy.wait_send()
    for k in range(1, n_row):
        for copy in x_copies(k):
            copy.wait_send()

    def z_drain(t, carry):
        mine = lax.rem(t, n_col) == me_c

        @pl.when(jnp.logical_not(mine))
        def _():
            z_copy(t).wait_send()

        @pl.when(mine)
        def _():
            def one(d, c2):
                a_copy(t, lax.rem(me_c + d, n_col)).wait_send()
                return c2

            lax.fori_loop(1, n_col, one, 0)

        return carry

    lax.fori_loop(0, n_t, z_drain, 0)

    def f_drain(t, carry):
        @pl.when(goes_on(t))
        def _():
            slot = jnp.where(t < n_gw, t, t - 2)
            for k in range(1, n_row):
                r = lax.rem(me_r + k, n_row)
                there = fx.at[r, slot]
                remote(there, there, f_s.at[t, r], f_r.at[r, t], row=r, col=me_c, ch=me).wait_recv()
                f_copy(t, k).wait_send()

        return carry

    lax.fori_loop(0, n_t, f_drain, 0)


def finish_kernel(dims, fx, v, gi, go, bias, vectors, conv):
    n_row, n_col, n_ch, cd, rows, chan, hid = dims
    hb = hid // n_ch // n_row
    n_gw = hb // 8 * 3
    hs = hid // n_ch
    factor = 1.0 / math.sqrt(rows * n_row * LANES * n_col)
    rest = chan - LANES
    g_in = []
    for r in range(n_row):
        for i in range(hb // 8):
            at = pl.ds(r * hb + 8 * i, 8)
            mixed = fx[r, 3 * i + 2] * factor
            g_in.append(jnp.concatenate([fx[r, 3 * i] * factor, mixed], axis=1))
            go[at, :LANES] = fx[r, 3 * i + 1] * factor
            go[at, LANES:] = mixed[:, 64 : 64 + rest]
    if hs % LANES:
        g_in.append(jnp.zeros((LANES - hs % LANES, 2 * LANES), F32))
    gi[...] = jnp.concatenate(g_in, axis=0).T[:chan, :hs]
    both = jnp.concatenate([v[0], v[1]], axis=1) * factor
    vectors[...] = both[:4, :chan]
    me = lax.axis_index("ch")
    row = jnp.zeros((1, hs), F32)
    flat = jnp.concatenate([both[4 + i : 5 + i, :chan] for i in range(hid // chan)], axis=1)
    for q in range(n_ch):
        row = jnp.where(me == q, flat[:, q * hs : (q + 1) * hs], row)
    bias[...] = row.reshape(hs)
    for i in range(cd // 8):
        total = fx[0, n_gw + i]
        for r in range(1, n_row):
            total = total + fx[r, n_gw + i]
        conv[pl.ds(8 * i, 8), :] = total[:, : KW * KW + 1] * factor


def run_block(dims, *args):
    n_row, n_col, n_ch, cd, rows, chan, hid = dims
    share = rows // n_ch
    chunks = share // 2
    blk = share * cd
    hb = hid // n_ch // n_row
    n_gw = hb // 8 * 3
    n_t = n_gw + 2 + cd // 8
    n_y = n_ch // 2
    pitch = -(-cd // 16) * 16
    n_tiles = rows // 32
    lanes_w = 3 * LANES
    padded = (rows + 2 * HALF) * cd
    vmem = lambda *shape: pltpu.VMEM(shape[:-1], shape[-1])
    dma = lambda *shape: pltpu.SemaphoreType.DMA(shape)
    two = lambda *shape: [dma(*shape), dma(*shape)]
    halo_bufs = [
        vmem(2, n_tiles, pitch, LANES, BF16),
        vmem(2, 4 * cd, LANES, BF16),
        vmem(2, n_tiles, pitch, LANES, BF16),
        vmem(2, 2, pitch, LANES, BF16),
    ]
    scratch = [
        vmem(rows * cd, LANES, F32),
        vmem(n_ch, blk, LANES, BF16),
        vmem(2, 4 * cd, LANES, BF16),
        vmem(2, 4 * cd, LANES, BF16),
        vmem(KW, padded, LANES, F32),
        vmem(KW, padded, LANES, F32),
        vmem(blk, LANES, F32),
        vmem(KW * KW * cd, LANES, F32),
        vmem(cd, LANES, F32),
        vmem(4, chan, LANES, F32),
        *halo_bufs,
        *halo_bufs,
        vmem(2, n_tiles + 2, cd, LANES, F32),
        vmem(n_ch, blk, LANES, BF16),
        vmem(n_ch, blk, LANES, BF16),
        vmem(n_ch, blk, LANES, BF16),
        vmem(n_ch, chunks, 4 * cd, LANES, BF16),
        vmem(n_ch, chunks, 4 * cd, LANES, BF16),
        vmem(chan + 64, hid, BF16),
        vmem(hid, chan + 64, BF16),
        vmem(hid, chan, BF16),
        vmem(hid, chan + 64, F32),
        vmem(hid, chan, F32),
        vmem(4, chan, LANES, F32),
        vmem(2, n_row, n_y * hb, lanes_w, BF16),
        vmem(n_row, n_y * hb, lanes_w, BF16),
        vmem(n_row, n_y * hb, lanes_w, BF16),
        vmem(n_row, n_y * hb, lanes_w, BF16),
        vmem(8, 2 * LANES, F32),
        vmem(8, 2 * LANES, F32),
        vmem(8, 2 * LANES, F32),
        vmem(n_row, 8, 2 * LANES, F32),
        vmem(n_y, hb, lanes_w, F32),
        vmem(n_y, hb, lanes_w, F32),
        vmem(8, 2 * LANES, F32),
        vmem(n_y, 8, 2 * LANES, F32),
        vmem((KW * KW + 1) * cd, LANES, F32),
        vmem(n_t, 8, LANES, F32),
        vmem(n_t, n_col, 8, LANES, F32),
        vmem(n_t, 8, LANES, F32),
        *two(8),
        *two(8),
        *two(n_ch),
        *two(n_ch),
        *two(n_ch, chunks),
        *two(2),
        *two(n_row),
        *two(n_row),
        *two(n_y),
        *two(n_y),
        dma(n_t),
        dma(n_t, n_col),
        dma(n_t, n_col),
        dma(n_t),
        dma(n_t, n_row),
        dma(n_row, n_t),
        pltpu.SemaphoreType.REGULAR((4,)),
    ]
    whole = pl.BlockSpec(memory_space=pltpu.VMEM)
    out, gin, fx, v = pl.pallas_call(
        functools.partial(block_kernel, dims),
        name="convnext_block",
        out_shape=(
            jax.ShapeDtypeStruct((rows * cd, LANES), BF16),
            jax.ShapeDtypeStruct((rows * cd, LANES), BF16),
            jax.ShapeDtypeStruct((n_row, n_gw + cd // 8, 8, LANES), F32),
            jax.ShapeDtypeStruct((2, 8, LANES), F32),
        ),
        in_specs=[whole] * len(args),
        out_specs=(whole,) * 4,
        scratch_shapes=scratch,
        compiler_params=pltpu.CompilerParams(
            collective_id=0, has_side_effects=True, vmem_limit_bytes=56 * 1024 * 1024
        ),
    )(*args)
    hs = hid // n_ch
    small = pl.pallas_call(
        functools.partial(finish_kernel, dims),
        name="finish",
        out_shape=(
            jax.ShapeDtypeStruct((chan, hs), F32),
            jax.ShapeDtypeStruct((hs, chan), F32),
            jax.ShapeDtypeStruct((hs,), F32),
            jax.ShapeDtypeStruct((4, chan), F32),
            jax.ShapeDtypeStruct((cd, KW * KW + 1), F32),
        ),
        in_specs=[whole] * 2,
        out_specs=(whole,) * 5,
    )(fx, v)
    return out, gin, small


def body(
    n_row,
    n_col,
    n_ch,
    features,
    cotangent,
    dw_kernel,
    dw_bias,
    ln_gain,
    ln_bias,
    w_in,
    in_bias,
    w_out,
    out_bias,
    layer_scale,
):
    cd, rows, wide = features.shape
    chan, hid = w_in.shape
    dims = (n_row, n_col, n_ch, cd, rows, chan, hid)
    vectors = (dw_bias, ln_gain, ln_bias, out_bias, layer_scale, in_bias)
    out, gin, small = run_block(dims, features, cotangent, dw_kernel, *vectors, w_in, w_out.T)
    g_in, g_out, g_bias, g_vectors, g_conv = small
    back = lambda v: v.reshape(rows, cd, wide).transpose(1, 0, 2)
    return back(out), back(gin), g_in, g_out, g_bias, g_vectors, g_conv


def solution(mesh):
    ch = P("ch", "row", "col")
    in_specs = (ch, ch, P("ch", None), P("ch")) + (P(),) * 7
    out_specs = (ch, ch, P(None, "ch"), P("ch", None), P("ch"), P(), P("ch", None))
    sizes = (mesh.shape["row"], mesh.shape["col"], mesh.shape["ch"])
    return jax.shard_map(
        functools.partial(body, *sizes), mesh=mesh, in_specs=in_specs, out_specs=out_specs, check_vma=False
    )
```

time: 112 us -> 82.2 us (0.73)
  Pallas kernels: 97.2 us -> 79.1 us
  local copies, waits for them, and re-layouts: 11.2 us -> 2.18 us
  other arithmetic: 2.2 us -> 0 us
    pallas_call x1, Pallas kernels: 97.2 us -> 77 us  [run_block(): pl.pallas_call(functools.partial(block_kernel, dims), name='convnext_bloc...]
    unnamed x26 -> x0, local copies, waits for them, and re-layouts: 3.72 us -> none
    transpose x2 -> x0, local copies, waits for them, and re-layouts: 3.05 us -> none  [the longest x1 2.05 us: body(): feat = features.transpose(1, 0, 2).reshape(rows * cd, wide)]
    pallas_call x0 -> x1, Pallas kernels: none -> 2.16 us  [run_block(): pl.pallas_call(functools.partial(finish_kernel, dims), name='finish', out...]
    mul x3 -> x0, other arithmetic: 1.53 us -> none  [the longest x1 0.93 us: body(): gw = gw * factor]
    broadcast_in_dim x2 -> x0, local copies, waits for them, and re-layouts: 1.26 us -> none  [the longest x1 0.68 us: body(): dw_bias[:, None]]
where the time goes in v1:
time: 82.2 us; the launch traced here: 82 us
  Pallas kernels  79.1 us (96%)
  local copies, waits for them, and re-layouts  2.18 us (3%)
    pallas_call x1, Pallas kernels, run_block(): pl.pallas_call(functools.partial(block_kernel, dims), name='convnext_bloc...  77 us
    transpose x1, local copies, waits for them, and re-layouts, body(): back = lambda v: v.reshape(rows, cd, wide).transpose(1, 0, 2)  2.18 us
    pallas_call x1, Pallas kernels, run_block(): pl.pallas_call(functools.partial(finish_kernel, dims), name='finish', out...  2.16 us

profile of v1, /device:TPU:6, one launch (start us, length us, event | category | flops | bytes accessed | tf_op | source)
XLA Modules:
  0.0 82.0 jit_solution(10752706542941074092)
XLA Ops:
  0.6 77.0 %convnext_block.1 = (bf16[1536,128]{1,0:T(8,128)(2,1)}, bf16[1536,128]{1,0:T(8,128)(2,1)}, f32[4,12,8,128]{3,2,1,0:T(8,128)}, f32[2,8,128]{2,1,0:T(8,128)}) custom-call(bf16[24,64,128]{2,1,0:T(8,128)(2,1)} %feat.1, bf16[24,64,128]{2,1,0:T(8,128)(2,1)} %cot.1, f32[24,49]{1,0:T(8,128)} %dw_kernel.1, f32[24]{0:T(128)} %dw_bias.1, f32[192]{0:T(256)} %ln_gain.1, ...), custom_call_target="tpu_custom_call" | custom-call | tf_op jit(solution)/shard_map/convnext_block/pallas_call | solution.py:856
  77.6 2.2 %copy_bitcast_fusion = (bf16[24,64,128]{2,1,0:T(8,128)(2,1)}, bf16[24,64,128]{2,1,0:T(8,128)(2,1)}) fusion(bf16[64,24,128]{2,1,0:T(8,128)(2,1)} %bitcast.8, bf16[64,24,128]{2,1,0:T(8,128)(2,1)} %bitcast.7), kind=kLoop, calls=%fused_computation | loop fusion | bytes 1572864 | tf_op jit(solution)/shard_map/transpose | solution.py:911
  79.8 2.2 %finish.1 = (f32[192,96]{1,0:T(8,128)}, f32[96,192]{1,0:T(8,128)}, f32[96]{0:T(128)}, f32[4,192]{1,0:T(4,128)}, f32[24,50]{1,0:T(8,128)}) custom-call(f32[4,12,8,128]{3,2,1,0:T(8,128)} %get-tuple-element.18.fx, f32[2,8,128]{2,1,0:T(8,128)} %get-tuple-element.19.v), custom_call_target="tpu_custom_call" | custom-call | tf_op jit(solution)/shard_map/finish/pallas_call | solution.py:873
